TPU v7x, 512 devices: a whole 4x4x16 slice. The times are simulated.
512 devices in a mesh: table: 16 (over x, y), replica: 32 (over z, core).
Axes of the slice: x: 4, y: 4, z: 16, core: 2. Of those that a mesh axis runs over, the one named last changes fastest.
Arguments:
- embeds: bfloat16 [131072, 512], P('replica', 'table'), may hold values from -6 to 6
- cotangent: bfloat16 [131072, 512], P('replica', 'table'), may hold values from -6 to 6
- send_plan: int32 [32, 16, 32], P('replica'), may hold values from 0 to 31, each once within a row
- work_plan: int32 [32, 16, 32], P('replica', 'table'), may hold values from 0 to 31, each once within a row
- sequence_tiles: int32 [32, 16, 4], P('replica', 'table'), may hold values from 1 to 16, 32 in all within a row
- slopes: float32 [8], replicated, may hold values from 0.002 to 0.2
- uvqk_weight: bfloat16 [512, 2048], replicated, may hold values from -0.25 to 0.25
- out_weight: bfloat16 [512, 512], replicated, may hold values from -0.25 to 0.25
Outputs:
- layer_output: bfloat16 [131072, 512], P('replica', 'table')
- input_gradient: bfloat16 [131072, 512], P('replica', 'table')
Inputs may be any that keep to these rules, and one draw needn't show every extreme that they name: `send_plan`: a device's 32 entries are all different. `work_plan`: a device's 32 entries are all different. `sequence_tiles`: a device's 4 entries sum to 32.
All inputs are finite; a program needn't handle non-finite values.
Results may differ from a plain program's by a relative error of at most 0.013.
Values may be sent and summed in bfloat16 or wider, within the bound.
No kernel may reach another device: no remote copies, remote signals or barrier semaphores. Data moves between devices by JAX's collectives and lax.ppermute only.
A program may use at most 64 MiB of HBM per device.

v0:
```python
import jax
import jax.numpy as jnp
from jax import lax
from jax.sharding import PartitionSpec as P

TILE = 8


EPSILON = 1e-05


def layer_norm(features):
    centre = jnp.mean(features, axis=-1, keepdims=True)
    centred = features - centre
    spread = jnp.mean(centred * centred, axis=-1, keepdims=True)
    return centred * lax.rsqrt(spread + EPSILON)


def segment_ids(lengths, row_count, tile_rows):
    boundary = jnp.cumsum(lengths)
    tile_index = jnp.arange(row_count, dtype=jnp.int32) // tile_rows
    return jnp.sum((tile_index[None, :] >= boundary[:, None]).astype(jnp.int32), axis=0)


def hstu_layer(inputs, segment, slopes, uvqk_weight, out_weight):
    row_count, feature_count = inputs.shape
    head_count = slopes.shape[0]
    head_size = feature_count // head_count
    score_scale = head_size ** (-0.5)
    normed = layer_norm(inputs.astype(jnp.float32)).astype(jnp.bfloat16)
    projected = jax.nn.silu(jnp.dot(normed, uvqk_weight, preferred_element_type=jnp.float32))
    gate_part = projected[:, :feature_count]
    value_part = projected[:, feature_count : 2 * feature_count].astype(jnp.bfloat16)
    query_part = projected[:, 2 * feature_count : 3 * feature_count].astype(jnp.bfloat16)
    key_part = projected[:, 3 * feature_count :].astype(jnp.bfloat16)
    row_index = lax.broadcasted_iota(jnp.int32, (row_count, row_count), 0)
    col_index = lax.broadcasted_iota(jnp.int32, (row_count, row_count), 1)
    allowed = (segment[:, None] == segment[None, :]) & (col_index <= row_index)
    distance = (row_index - col_index).astype(jnp.float32)
    pieces = []
    for head_index in range(head_count):
        lower = head_index * head_size
        upper = lower + head_size
        scores = jnp.dot(
            query_part[:, lower:upper],
            key_part[:, lower:upper].T,
            preferred_element_type=jnp.float32,
        )
        scores = scores * score_scale - slopes[head_index] * distance
        weights = jnp.where(allowed, jax.nn.silu(scores), jnp.zeros_like(scores)).astype(
            jnp.bfloat16
        )
        pieces.append(
            jnp.dot(weights, value_part[:, lower:upper], preferred_element_type=jnp.float32)
        )
    attended = jnp.concatenate(pieces, axis=1)
    gated = (layer_norm(attended) * gate_part).astype(jnp.bfloat16)
    mixing = jnp.dot(gated, out_weight, preferred_element_type=jnp.float32)
    return (inputs.astype(jnp.float32) + mixing).astype(jnp.bfloat16)


def forward_backward(inputs, grad_rows, segment, slopes, uvqk_weight, out_weight):

    def apply_layer(layer_input):
        return hstu_layer(layer_input, segment, slopes, uvqk_weight, out_weight)

    outputs, pullback = jax.vjp(apply_layer, inputs)
    return (outputs, pullback(grad_rows)[0])


def shards(
    embeds, cotangent, send_plan, work_plan, sequence_tiles, slopes, uvqk_weight, out_weight
):
    table_count = lax.axis_size("table")
    replica_count = lax.axis_size("replica")
    column_count = embeds.shape[1]
    row_count = embeds.shape[0] // table_count
    tile_count = row_count // TILE
    peer_rows = row_count // replica_count
    feature_count = column_count * table_count
    block_plans = send_plan[0]
    own_send = lax.dynamic_index_in_dim(block_plans, lax.axis_index("table"), 0, keepdims=False)
    own_work = work_plan[0, 0]
    segment = segment_ids(sequence_tiles[0, 0], row_count, TILE)
    tile_order = jnp.arange(tile_count, dtype=jnp.int32)
    row_inputs, row_grads = (
        lax.all_to_all(embeds, "table", split_axis=0, concat_axis=1, tiled=True),
        lax.all_to_all(cotangent, "table", split_axis=0, concat_axis=1, tiled=True),
    )

    def to_slots(shard_rows):
        tiled = shard_rows.reshape(tile_count, TILE, feature_count)
        return tiled[own_send]

    got_inputs, got_grads = (
        lax.all_to_all(to_slots(row_inputs), "replica", split_axis=0, concat_axis=0, tiled=True),
        lax.all_to_all(to_slots(row_grads), "replica", split_axis=0, concat_axis=0, tiled=True),
    )
    work_inputs = got_inputs[own_work].reshape(row_count, feature_count)
    work_grads = got_grads[own_work].reshape(row_count, feature_count)
    outputs, gradient = forward_backward(
        work_inputs, work_grads, segment, slopes, uvqk_weight, out_weight
    )
    undo_work = jnp.zeros((tile_count,), jnp.int32).at[own_work].set(tile_order)

    def to_sources(result):
        return result.reshape(tile_count, TILE, feature_count)[undo_work]

    slot_outputs = to_sources(outputs)
    slot_grads = to_sources(gradient)
    back_outputs, back_grads = (
        lax.all_to_all(slot_outputs, "replica", split_axis=0, concat_axis=0, tiled=True),
        lax.all_to_all(slot_grads, "replica", split_axis=0, concat_axis=0, tiled=True),
    )
    undo_send = jnp.zeros((tile_count,), jnp.int32).at[own_send].set(tile_order)

    def to_home(result):
        return result[undo_send].reshape(row_count, feature_count)

    layer_output, input_gradient = (
        lax.all_to_all(to_home(back_outputs), "table", split_axis=1, concat_axis=0, tiled=True),
        lax.all_to_all(to_home(back_grads), "table", split_axis=1, concat_axis=0, tiled=True),
    )
    return (layer_output, input_gradient)


def solution(mesh):
    in_specs = (
        P("replica", "table"),
        P("replica", "table"),
        P("replica", None, None),
        P("replica", "table", None),
        P("replica", "table", None),
        P(),
        P(),
        P(),
    )
    out_specs = (P("replica", "table"), P("replica", "table"))
    return jax.shard_map(shards, mesh=mesh, in_specs=in_specs, out_specs=out_specs, check_vma=False)
```

profile of v0, /device:TPU:1, one launch (start us, length us, event | category | flops | bytes accessed | tf_op | source)
XLA Modules:
  0.0 188.0 jit_solution(13173466169853847524)
XLA Ops:
  0.6 1.8 copy.253
  2.5 7.6 %all-to-all-start = ((bf16[16,256,32]{1,2,0:T(8,128)(2,1)}), bf16[16,256,32]{1,2,0:T(8,128)(2,1)S(1)}, u32[]{:S(2)}, u32[]{:S(2)}) async-start(bf16[16,256,32]{1,2,0:T(8,128)(2,1)} %bitcast.104), calls=%async_computation | async-start | bytes 524288 | tf_op jit(solution)/shard_map/all_to_all | solution.py:87
  10.1 1.7 copy.252
  11.7 5.7 %all-to-all-done = bf16[16,256,32]{1,2,0:T(8,128)(2,1)S(1)} async-done(((bf16[16,256,32]{1,2,0:T(8,128)(2,1)}), bf16[16,256,32]{1,2,0:T(8,128)(2,1)S(1)}, u32[]{:S(2)}, u32[]{:S(2)}) %all-to-all-start) | async-done | bytes 262176 | tf_op jit(solution)/shard_map/all_to_all | solution.py:87
  17.4 4.3 %all-to-all-start.4 = ((bf16[16,256,32]{1,2,0:T(8,128)(2,1)}), bf16[16,256,32]{1,2,0:T(8,128)(2,1)}, u32[]{:S(2)}, u32[]{:S(2)}) async-start(bf16[16,256,32]{1,2,0:T(8,128)(2,1)} %bitcast.103), calls=%async_computation.4 | async-start | bytes 524288 | tf_op jit(solution)/shard_map/all_to_all | solution.py:88
  21.8 0.7 fusion.166
  23.0 0.9 copy.233
  24.0 1.0 reshape.225
  25.0 1.3 gather_fusion
  26.3 2.8 %all-to-all-done.4 = bf16[16,256,32]{1,2,0:T(8,128)(2,1)} async-done(((bf16[16,256,32]{1,2,0:T(8,128)(2,1)}), bf16[16,256,32]{1,2,0:T(8,128)(2,1)}, u32[]{:S(2)}, u32[]{:S(2)}) %all-to-all-start.4) | async-done | bytes 262176 | tf_op jit(solution)/shard_map/all_to_all | solution.py:88
  29.1 18.6 %all-to-all-start.1 = ((bf16[32,8,512]{2,1,0:T(8,128)(2,1)}), bf16[32,8,512]{2,1,0:T(8,128)(2,1)}, u32[]{:S(2)}, u32[]{:S(2)}) async-start(bf16[32,8,512]{2,1,0:T(8,128)(2,1)} %gather_fusion), calls=%async_computation.1 | async-start | bytes 524288 | tf_op jit(solution)/shard_map/all_to_all | solution.py:96
  49.9 1.9 %copy.239 = bf16[256,16,32]{2,1,0:T(8,128)(2,1)S(1)} copy(bf16[256,16,32]{0,2,1:T(8,128)(2,1)} %bitcast.18) | data formatting | bytes 524288 | tf_op jit(solution)/shard_map/all_to_all | solution.py:88
  51.8 1.0 reshape.229
  52.8 1.3 gather_fusion.4
  54.1 15.9 %all-to-all-done.1 = bf16[32,8,512]{2,1,0:T(8,128)(2,1)} async-done(((bf16[32,8,512]{2,1,0:T(8,128)(2,1)}), bf16[32,8,512]{2,1,0:T(8,128)(2,1)}, u32[]{:S(2)}, u32[]{:S(2)}) %all-to-all-start.1) | async-done | bytes 262176 | tf_op jit(solution)/shard_map/all_to_all | solution.py:96
  70.0 4.2 %all-to-all-start.5 = ((bf16[32,8,512]{2,1,0:T(8,128)(2,1)}), bf16[32,8,512]{2,1,0:T(8,128)(2,1)S(1)}, u32[]{:S(2)}, u32[]{:S(2)}) async-start(bf16[32,8,512]{2,1,0:T(8,128)(2,1)} %gather_fusion.4), calls=%async_computation.5 | async-start | bytes 524288 | tf_op jit(solution)/shard_map/all_to_all | solution.py:97
  74.2 1.5 gather_fusion.1
  76.3 3.1 %fusion.177 = (bf16[256,2048]{0,1:T(8,128)(2,1)S(1)}, f32[256,2048]{0,1:T(8,128)}, f32[256,2048]{0,1:T(8,128)}) fusion(bf16[512,2048]{1,0:T(8,128)(2,1)S(1)} %copy-done, bf16[32,8,512]{2,1,0:T(8,128)(2,1)S(1)} %gather_fusion.1, f32[256]{0:T(256)S(1)} %rsqrt.20, f32[256]{0:T(256)S(1)} %div.78), kind=kOutput, calls=%fused_computation.297 | convolution fusion | flops 540016640 | bytes 7604224 | tf_op jit(solution)/shard_map/jvp()/dot_general | solution.py:31
  79.4 0.8 fusion.23
  80.2 0.9 fusion.24
  81.1 0.8 fusion.25
  81.9 0.9 fusion.26
  82.8 0.8 fusion.27
  83.6 0.9 fusion.28
  84.5 0.9 fusion.29
  85.5 1.8 select_convert_fusion
  89.1 6.7 %all-to-all-done.5 = bf16[32,8,512]{2,1,0:T(8,128)(2,1)S(1)} async-done(((bf16[32,8,512]{2,1,0:T(8,128)(2,1)}), bf16[32,8,512]{2,1,0:T(8,128)(2,1)S(1)}, u32[]{:S(2)}, u32[]{:S(2)}) %all-to-all-start.5) | async-done | bytes 262176 | tf_op jit(solution)/shard_map/all_to_all | solution.py:97
  96.4 1.5 multiply_reduce_fusion
  98.0 1.3 fusion.176
  107.1 1.3 fusion.56
  109.0 1.4 gather_fusion.6
  110.4 5.6 %all-to-all-start.6 = ((bf16[32,8,512]{2,1,0:T(8,128)(2,1)}), bf16[32,8,512]{2,1,0:T(8,128)(2,1)S(1)}, u32[]{:S(2)}, u32[]{:S(2)}) async-start(bf16[32,8,512]{2,1,0:T(8,128)(2,1)} %gather_fusion.6), calls=%async_computation.6 | async-start | bytes 524288 | tf_op jit(solution)/shard_map/all_to_all | solution.py:113
  116.0 1.5 fusion.30
  117.5 1.4 gather_fusion.2
  118.9 19.3 %all-to-all-done.6 = bf16[32,8,512]{2,1,0:T(8,128)(2,1)S(1)} async-done(((bf16[32,8,512]{2,1,0:T(8,128)(2,1)}), bf16[32,8,512]{2,1,0:T(8,128)(2,1)S(1)}, u32[]{:S(2)}, u32[]{:S(2)}) %all-to-all-start.6) | async-done | bytes 262176 | tf_op jit(solution)/shard_map/all_to_all | solution.py:113
  138.2 4.8 %all-to-all-start.2 = ((bf16[32,8,512]{2,1,0:T(8,128)(2,1)}), bf16[32,8,512]{2,1,0:T(8,128)(2,1)}, u32[]{:S(2)}, u32[]{:S(2)}) async-start(bf16[32,8,512]{2,1,0:T(8,128)(2,1)} %gather_fusion.2), calls=%async_computation.2 | async-start | bytes 524288 | tf_op jit(solution)/shard_map/all_to_all | solution.py:112
  143.1 0.8 scatter_custom_fusion.1
  143.9 1.5 gather_fusion.7
  146.0 1.5 copy.242
  147.6 17.2 %all-to-all-done.2 = bf16[32,8,512]{2,1,0:T(8,128)(2,1)} async-done(((bf16[32,8,512]{2,1,0:T(8,128)(2,1)}), bf16[32,8,512]{2,1,0:T(8,128)(2,1)}, u32[]{:S(2)}, u32[]{:S(2)}) %all-to-all-start.2) | async-done | bytes 262176 | tf_op jit(solution)/shard_map/all_to_all | solution.py:112
  164.7 4.2 %all-to-all-start.7 = ((bf16[256,16,32]{0,2,1:T(8,128)(2,1)}), bf16[256,16,32]{0,2,1:T(8,128)(2,1)}, u32[]{:S(2)}, u32[]{:S(2)}) async-start(bf16[256,16,32]{0,2,1:T(8,128)(2,1)} %copy.242), calls=%async_computation.7 | async-start | bytes 524288 | tf_op jit(solution)/shard_map/all_to_all | solution.py:122
  168.9 1.5 gather_fusion.3
  171.1 1.6 copy.236
  172.6 3.7 %all-to-all-done.7 = bf16[256,16,32]{0,2,1:T(8,128)(2,1)} async-done(((bf16[256,16,32]{0,2,1:T(8,128)(2,1)}), bf16[256,16,32]{0,2,1:T(8,128)(2,1)}, u32[]{:S(2)}, u32[]{:S(2)}) %all-to-all-start.7) | async-done | bytes 262176 | tf_op jit(solution)/shard_map/all_to_all | solution.py:122
  176.3 3.7 %all-to-all-start.3 = ((bf16[256,16,32]{0,2,1:T(8,128)(2,1)}), bf16[256,16,32]{0,2,1:T(8,128)(2,1)S(1)}, u32[]{:S(2)}, u32[]{:S(2)}) async-start(bf16[256,16,32]{0,2,1:T(8,128)(2,1)} %copy.236), calls=%async_computation.3 | async-start | bytes 524288 | tf_op jit(solution)/shard_map/all_to_all | solution.py:121
  180.0 1.7 copy.249
  181.6 5.7 %all-to-all-done.3 = bf16[256,16,32]{0,2,1:T(8,128)(2,1)S(1)} async-done(((bf16[256,16,32]{0,2,1:T(8,128)(2,1)}), bf16[256,16,32]{0,2,1:T(8,128)(2,1)S(1)}, u32[]{:S(2)}, u32[]{:S(2)}) %all-to-all-start.3) | async-done | bytes 262176 | tf_op jit(solution)/shard_map/all_to_all | solution.py:121
  187.3 0.7 copy.248
  (158 shorter events, 14.8 us)
Async XLA Ops:
  0.6 75.6 %copy-start = (bf16[512,2048]{1,0:T(8,128)(2,1)S(1)}, bf16[512,2048]{1,0:T(8,128)(2,1)}, u32[]{:S(2)}) copy-start(bf16[512,2048]{1,0:T(8,128)(2,1)} %param.14) | copy-start | bytes 6291460
  2.5 14.9 %all-to-all-start = ((bf16[16,256,32]{1,2,0:T(8,128)(2,1)}), bf16[16,256,32]{1,2,0:T(8,128)(2,1)S(1)}, u32[]{:S(2)}, u32[]{:S(2)}) async-start(bf16[16,256,32]{1,2,0:T(8,128)(2,1)} %bitcast.104), calls=%async_computation | async-start | bytes 524288 | tf_op jit(solution)/shard_map/all_to_all | solution.py:87
  17.4 30.2 %copy-start.24 = (s32[1,1,4]{2,1,0:T(1,128)S(1)}, s32[1,1,4]{2,1,0:T(1,128)}, u32[]{:S(2)}) copy-start(s32[1,1,4]{2,1,0:T(1,128)} %param.12) | copy-start | bytes 52
  17.4 30.4 %copy-start.25 = (s32[1,1,32]{2,1,0:T(1,128)S(1)}, s32[1,1,32]{2,1,0:T(1,128)}, u32[]{:S(2)}) copy-start(s32[1,1,32]{2,1,0:T(1,128)} %param.11) | copy-start | bytes 388
  17.4 31.7 %copy-start.18 = (f32[8]{0:T(128)S(1)}, f32[8]{0:T(128)}, u32[]{:S(2)}) copy-start(f32[8]{0:T(128)} %param.13) | copy-start | bytes 100
  17.4 11.7 %all-to-all-start.4 = ((bf16[16,256,32]{1,2,0:T(8,128)(2,1)}), bf16[16,256,32]{1,2,0:T(8,128)(2,1)}, u32[]{:S(2)}, u32[]{:S(2)}) async-start(bf16[16,256,32]{1,2,0:T(8,128)(2,1)} %bitcast.103), calls=%async_computation.4 | async-start | bytes 524288 | tf_op jit(solution)/shard_map/all_to_all | solution.py:88
  29.1 40.9 %all-to-all-start.1 = ((bf16[32,8,512]{2,1,0:T(8,128)(2,1)}), bf16[32,8,512]{2,1,0:T(8,128)(2,1)}, u32[]{:S(2)}, u32[]{:S(2)}) async-start(bf16[32,8,512]{2,1,0:T(8,128)(2,1)} %gather_fusion), calls=%async_computation.1 | async-start | bytes 524288 | tf_op jit(solution)/shard_map/all_to_all | solution.py:96
  49.9 35.5 %copy-start.21 = (s32[256]{0:T(256)}, s32[256]{0:T(256)S(1)}, u32[]{:S(2)}) copy-start(s32[256]{0:T(256)S(1)} %convert_reduce_fusion.1) | copy-start | bytes 3076
  70.0 25.9 %all-to-all-start.5 = ((bf16[32,8,512]{2,1,0:T(8,128)(2,1)}), bf16[32,8,512]{2,1,0:T(8,128)(2,1)S(1)}, u32[]{:S(2)}, u32[]{:S(2)}) async-start(bf16[32,8,512]{2,1,0:T(8,128)(2,1)} %gather_fusion.4), calls=%async_computation.5 | async-start | bytes 524288 | tf_op jit(solution)/shard_map/all_to_all | solution.py:97
  76.2 3.2 %copy-start.19 = (f32[256]{0:T(256)}, f32[256]{0:T(256)S(1)}, u32[]{:S(2)}) copy-start(f32[256]{0:T(256)S(1)} %add.156) | copy-start | bytes 3076
  79.4 9.5 %copy-start.2 = (bf16[256,2048]{0,1:T(8,128)(2,1)}, bf16[256,2048]{0,1:T(8,128)(2,1)S(1)}, u32[]{:S(2)}) copy-start(bf16[256,2048]{0,1:T(8,128)(2,1)S(1)} %get-tuple-element.6) | copy-start | bytes 3145732
  80.2 7.1 %copy-start.26 = (f32[256,256]{1,0:T(8,128)}, f32[256,256]{1,0:T(8,128)S(1)}, u32[]{:S(2)}) copy-start(f32[256,256]{1,0:T(8,128)S(1)} %fusion.23) | copy-start | bytes 786436
  81.1 6.2 %copy-start.28 = (f32[256,256]{1,0:T(8,128)}, f32[256,256]{1,0:T(8,128)S(1)}, u32[]{:S(2)}) copy-start(f32[256,256]{1,0:T(8,128)S(1)} %fusion.24) | copy-start | bytes 786436
  81.9 5.4 %copy-start.30 = (f32[256,256]{1,0:T(8,128)}, f32[256,256]{1,0:T(8,128)S(1)}, u32[]{:S(2)}) copy-start(f32[256,256]{1,0:T(8,128)S(1)} %fusion.25) | copy-start | bytes 786436
  82.8 4.5 %copy-start.32 = (f32[256,256]{1,0:T(8,128)}, f32[256,256]{1,0:T(8,128)S(1)}, u32[]{:S(2)}) copy-start(f32[256,256]{1,0:T(8,128)S(1)} %fusion.26) | copy-start | bytes 786436
  83.6 3.7 %copy-start.34 = (f32[256,256]{1,0:T(8,128)}, f32[256,256]{1,0:T(8,128)S(1)}, u32[]{:S(2)}) copy-start(f32[256,256]{1,0:T(8,128)S(1)} %fusion.27) | copy-start | bytes 786436
  84.5 2.8 %copy-start.36 = (f32[256,256]{1,0:T(8,128)}, f32[256,256]{1,0:T(8,128)S(1)}, u32[]{:S(2)}) copy-start(f32[256,256]{1,0:T(8,128)S(1)} %fusion.28) | copy-start | bytes 786436
  85.4 1.9 copy-start.38
  87.3 1.7 copy-start.8
  87.3 1.7 copy-start.10
  87.3 1.7 copy-start.12
  87.3 1.7 copy-start.14
  87.4 1.7 copy-start.16
  87.4 1.8 copy-start.4
  87.4 1.8 copy-start.6
  98.0 1.4 copy-start.3
  98.0 1.4 copy-start.22
  98.0 1.4 copy-start.27
  98.0 1.7 copy-start.29
  99.7 1.0 copy-start.33
  100.4 1.0 copy-start.35
  100.7 1.0 copy-start.37
  101.4 1.0 copy-start.39
  101.7 1.0 copy-start.40
  102.6 3.1 %copy-start.17 = (bf16[256,256]{1,0:T(8,128)(2,1)S(1)}, bf16[256,256]{1,0:T(8,128)(2,1)}, u32[]{:S(2)}) copy-start(bf16[256,256]{1,0:T(8,128)(2,1)} %copy-done.16) | copy-start | bytes 393220
  102.9 3.0 %copy-start.15 = (bf16[256,256]{1,0:T(8,128)(2,1)S(1)}, bf16[256,256]{1,0:T(8,128)(2,1)}, u32[]{:S(2)}) copy-start(bf16[256,256]{1,0:T(8,128)(2,1)} %copy-done.14) | copy-start | bytes 393220
  102.9 3.1 %copy-start.13 = (bf16[256,256]{1,0:T(8,128)(2,1)S(1)}, bf16[256,256]{1,0:T(8,128)(2,1)}, u32[]{:S(2)}) copy-start(bf16[256,256]{1,0:T(8,128)(2,1)} %copy-done.12) | copy-start | bytes 393220
  102.9 3.3 %copy-start.11 = (bf16[256,256]{1,0:T(8,128)(2,1)S(1)}, bf16[256,256]{1,0:T(8,128)(2,1)}, u32[]{:S(2)}) copy-start(bf16[256,256]{1,0:T(8,128)(2,1)} %copy-done.10) | copy-start | bytes 393220
  102.9 3.4 %copy-start.9 = (bf16[256,256]{1,0:T(8,128)(2,1)S(1)}, bf16[256,256]{1,0:T(8,128)(2,1)}, u32[]{:S(2)}) copy-start(bf16[256,256]{1,0:T(8,128)(2,1)} %copy-done.8) | copy-start | bytes 393220
  102.9 3.6 %copy-start.7 = (bf16[256,256]{1,0:T(8,128)(2,1)S(1)}, bf16[256,256]{1,0:T(8,128)(2,1)}, u32[]{:S(2)}) copy-start(bf16[256,256]{1,0:T(8,128)(2,1)} %copy-done.6) | copy-start | bytes 393220
  103.1 3.6 %copy-start.5 = (bf16[256,256]{1,0:T(8,128)(2,1)S(1)}, bf16[256,256]{1,0:T(8,128)(2,1)}, u32[]{:S(2)}) copy-start(bf16[256,256]{1,0:T(8,128)(2,1)} %copy-done.4) | copy-start | bytes 393220
  104.8 2.3 %copy-start.41 = (f32[256,2048]{0,1:T(8,128)S(1)}, f32[256,2048]{0,1:T(8,128)}, u32[]{:S(2)}) copy-start(f32[256,2048]{0,1:T(8,128)} %get-tuple-element.43) | copy-start | bytes 6291460
  107.1 1.3 copy-start.20
  110.4 27.8 %all-to-all-start.6 = ((bf16[32,8,512]{2,1,0:T(8,128)(2,1)}), bf16[32,8,512]{2,1,0:T(8,128)(2,1)S(1)}, u32[]{:S(2)}, u32[]{:S(2)}) async-start(bf16[32,8,512]{2,1,0:T(8,128)(2,1)} %gather_fusion.6), calls=%async_computation.6 | async-start | bytes 524288 | tf_op jit(solution)/shard_map/all_to_all | solution.py:113
  138.2 5.7 %copy-start.1 = (bf16[32,8,512]{2,1,0:T(8,128)(2,1)}, bf16[32,8,512]{2,1,0:T(8,128)(2,1)S(1)}, u32[]{:S(2)}) copy-start(bf16[32,8,512]{2,1,0:T(8,128)(2,1)S(1)} %all-to-all-done.6) | copy-start | bytes 786436
  138.2 26.5 %all-to-all-start.2 = ((bf16[32,8,512]{2,1,0:T(8,128)(2,1)}), bf16[32,8,512]{2,1,0:T(8,128)(2,1)}, u32[]{:S(2)}, u32[]{:S(2)}) async-start(bf16[32,8,512]{2,1,0:T(8,128)(2,1)} %gather_fusion.2), calls=%async_computation.2 | async-start | bytes 524288 | tf_op jit(solution)/shard_map/all_to_all | solution.py:112
  164.7 11.5 %all-to-all-start.7 = ((bf16[256,16,32]{0,2,1:T(8,128)(2,1)}), bf16[256,16,32]{0,2,1:T(8,128)(2,1)}, u32[]{:S(2)}, u32[]{:S(2)}) async-start(bf16[256,16,32]{0,2,1:T(8,128)(2,1)} %copy.242), calls=%async_computation.7 | async-start | bytes 524288 | tf_op jit(solution)/shard_map/all_to_all | solution.py:122
  176.3 11.0 %all-to-all-start.3 = ((bf16[256,16,32]{0,2,1:T(8,128)(2,1)}), bf16[256,16,32]{0,2,1:T(8,128)(2,1)S(1)}, u32[]{:S(2)}, u32[]{:S(2)}) async-start(bf16[256,16,32]{0,2,1:T(8,128)(2,1)} %copy.236), calls=%async_computation.3 | async-start | bytes 524288 | tf_op jit(solution)/shard_map/all_to_all | solution.py:121
  (2 other events, 1.5 us)
where the time goes:
time: 190 us; the launch traced here: 188 us
  waiting for transfers between devices  76.9 us (40%)
  starting transfers between devices  52.9 us (28%)
  local copies, waits for them, and re-layouts  29.8 us (16%)
  matrix products  22.9 us (12%)
  other arithmetic  3.92 us (2%)
    all_to_all x1, waiting for transfers between devices, shards(): lax.all_to_all(slot_grads, 'replica', split_axis=0, concat_axis=0, tiled=...  19.3 us
    all_to_all x1, starting transfers between devices, shards(): lax.all_to_all(to_slots(row_inputs), 'replica', split_axis=0, concat_axis...  18.6 us
    all_to_all x1, waiting for transfers between devices, shards(): lax.all_to_all(slot_outputs, 'replica', split_axis=0, concat_axis=0, tile...  17.2 us
    all_to_all x1, waiting for transfers between devices, shards(): lax.all_to_all(to_slots(row_inputs), 'replica', split_axis=0, concat_axis...  15.9 us
    dot_general x24, matrix products, hstu_layer(): jnp.dot(query_part[:, lower:upper], key_part[:, lower:upper].T, preferred...  10.5 us
    all_to_all x1, starting transfers between devices, shards(): lax.all_to_all(embeds, 'table', split_axis=0, concat_axis=1, tiled=True)  7.57 us
    all_to_all x1, waiting for transfers between devices, shards(): lax.all_to_all(to_slots(row_grads), 'replica', split_axis=0, concat_axis=...  6.71 us
    all_to_all x1, waiting for transfers between devices, shards(): lax.all_to_all(embeds, 'table', split_axis=0, concat_axis=1, tiled=True)  5.69 us
  transfers between devices with their start and end apart: 8, of which 8 were waited for; matrix products, arithmetic and copies ran while one was open for 20% of the time, Pallas kernels for 0%

commit v1 on v0

v1 whole, which is shorter than its diff:
```python
import jax
import jax.numpy as jnp
from jax import lax
from jax.experimental import pallas as pl
from jax.experimental.pallas import tpu as pltpu
from jax.sharding import PartitionSpec as P

TILE = 8
HALF = 4
EPSILON = 1e-05
BF16 = jnp.bfloat16
F32 = jnp.float32
FAR = 1e30


def dot(a, b, ca=1, cb=0):
    return lax.dot_general(a, b, (((ca,), (cb,)), ((), ())), preferred_element_type=F32)


def one_hot(rows, target):
    index = lax.broadcasted_iota(jnp.int32, (rows, target.shape[1]), 0)
    return jnp.where(index == target, 1.0, 0.0).astype(BF16)


def spread(plan, repeat):
    slots = plan.shape[1]
    lanes = slots * repeat
    slot = lax.broadcasted_iota(jnp.int32, (slots, lanes), 0)
    lane = lax.broadcasted_iota(jnp.int32, (slots, lanes), 1)
    pick = jnp.where(lane // repeat == slot, 1.0, 0.0).astype(BF16)
    return dot(plan.astype(F32).astype(BF16), pick).astype(jnp.int32)


def lane_index(lanes):
    return lax.broadcasted_iota(jnp.int32, (1, lanes), 1)


def to_blocks(top, bottom):
    m = top.shape[1] // 2
    return jnp.concatenate([top[:, :m], bottom[:, :m], top[:, m:], bottom[:, m:]], axis=0).T


def from_blocks(block):
    turned = block.T
    c2 = turned.shape[0] // 2
    return jnp.concatenate([turned[:c2], turned[c2:]], axis=1)


def send_kernel(plan_ref, x_ref, g_ref, out_ref):
    tables, peers = plan_ref.shape
    rows = peers * TILE
    m = peers * HALF
    lane = lane_index(m)
    base = spread(plan_ref[...], HALF) * TILE + lane % HALF
    target = jnp.concatenate([base, base + HALF], axis=1)
    for t in range(tables):
        pick = one_hot(rows, target[t : t + 1])
        span = pl.ds(t * rows, rows)
        top = dot(x_ref[:, span], pick).astype(BF16)
        bottom = dot(g_ref[:, span], pick).astype(BF16)
        out_ref[pl.ds(t * m, m), :] = to_blocks(top, bottom)


def home_kernel(back_ref, in_ref, y_ref, d_ref):
    tables, peers = back_ref.shape
    rows = peers * TILE
    m = peers * HALF
    lane = lane_index(rows)
    inner = lane % TILE
    target = spread(back_ref[...], TILE) * HALF + inner % HALF + (inner // HALF) * m
    c = y_ref.shape[0]
    for t in range(tables):
        place = one_hot(2 * m, target[t : t + 1])
        span = pl.ds(t * rows, rows)
        got = dot(from_blocks(in_ref[pl.ds(t * m, m), :]), place).astype(BF16)
        y_ref[:, span] = got[:c]
        d_ref[:, span] = got[c:]


def norm_parts(x):
    n = x.shape[0]
    centred = x - jnp.sum(x, axis=0, keepdims=True) * (1.0 / n)
    spread_ = jnp.sum(centred * centred, axis=0, keepdims=True) * (1.0 / n)
    inv = lax.rsqrt(spread_ + EPSILON)
    return centred * inv, inv


def norm_back(grad, normed, inv):
    n = grad.shape[0]
    mean = jnp.sum(grad, axis=0, keepdims=True) * (1.0 / n)
    along = jnp.sum(grad * normed, axis=0, keepdims=True) * (1.0 / n)
    return inv * (grad - mean - normed * along)


def layer_kernel(
    slopes_ref, in_ref, pick_ref, place_ref, far_ref, wt_ref, w_ref, ot_ref, o_ref, out_ref,
    x_ref, g_ref, slope_ref, gate_ref, v_ref, q_ref, k_ref, w8_ref, d8_ref, att_ref, dp_ref,
    y_ref, dx_ref,
):
    features, rows = x_ref.shape
    heads = slopes_ref.shape[0]
    size = features // heads
    tables = in_ref.shape[0] // (rows // 2)
    m = rows // 2
    c = features // tables
    for t in range(tables):
        both = from_blocks(in_ref[pl.ds(t * m, m), :])
        x_ref[pl.ds(t * c, c), :] = both[:c]
        g_ref[pl.ds(t * c, c), :] = both[c:]
    pick = pick_ref[...]
    x = dot(x_ref[...], pick)
    g = dot(g_ref[...], pick)
    x_ref[...] = x.astype(BF16)
    g_ref[...] = g.astype(BF16)
    normed, inv = norm_parts(x)
    sent = normed.astype(BF16)

    step = 256
    scale = size ** (-0.5)
    for part in range(0, 4 * features, step):
        half = dot(wt_ref[pl.ds(part, step), :], sent)
        bend = jnp.tanh(half)
        act = half + half * bend
        slope_ref[pl.ds(part, step), :] = (1.0 + bend) * (1.0 + half * (1.0 - bend))
        at = pl.ds(part % features, step)
        kind = part // features
        if kind == 0:
            gate_ref[at, :] = act
        elif kind == 1:
            v_ref[at, :] = act.astype(BF16)
        elif kind == 2:
            q_ref[at, :] = (act * (scale * 0.5)).astype(BF16)
        else:
            k_ref[at, :] = act.astype(BF16)

    row = lax.broadcasted_iota(jnp.int32, (m, rows), 0)
    col = lax.broadcasted_iota(jnp.int32, (m, rows), 1)
    apart = (col - row).astype(F32)
    for h in range(heads):
        at = pl.ds(h * size, size)
        slope = slopes_ref[h] * 0.5
        for b in range(2):
            keys = pl.ds(b * m, m)
            asks = pl.ds(b * m, rows - b * m)
            dist = apart[:, : rows - b * m]
            half = dot(k_ref[at, keys], q_ref[at, asks], 0, 0)
            half = (half - far_ref[keys, asks]) - slope * dist
            bend = jnp.tanh(half)
            w8_ref[h, keys, asks] = (half + half * bend).astype(BF16)
            d8_ref[h, keys, asks] = (1.0 + bend) * (1.0 + half * (1.0 - bend))
        low = dot(v_ref[at, :], w8_ref[h, :, pl.ds(m, m)])
        att_ref[at, pl.ds(m, m)] = low
        att_ref[at, pl.ds(0, m)] = dot(v_ref[at, pl.ds(0, m)], w8_ref[h, pl.ds(0, m), pl.ds(0, m)])

    gate = gate_ref[...]
    even, inv_a = norm_parts(att_ref[...])
    gated = (even * gate).astype(BF16)
    y_ref[...] = (x_ref[...].astype(F32) + dot(ot_ref[...], gated)).astype(BF16)

    d_gated = dot(o_ref[...], g_ref[...]).astype(BF16).astype(F32)
    dp_ref[pl.ds(0, features), :] = (d_gated * even * slope_ref[pl.ds(0, features), :]).astype(BF16)
    att_ref[...] = norm_back(d_gated * gate, even, inv_a)
    for h in range(heads):
        at = pl.ds(h * size, size)
        d_att = att_ref[at, :].astype(BF16)
        v = v_ref[at, :]
        k = k_ref[at, :]
        q = q_ref[at, :]
        top = dot(v[:, :m], d_att, 0, 0) * d8_ref[h, pl.ds(0, m), :]
        low = dot(v[:, m:], d_att[:, m:], 0, 0) * d8_ref[h, pl.ds(m, m), pl.ds(m, m)]
        top = top.astype(BF16)
        low = low.astype(BF16)
        dv0 = dot(d_att, w8_ref[h, pl.ds(0, m), :], 1, 1)
        dv1 = dot(d_att[:, m:], w8_ref[h, pl.ds(m, m), pl.ds(m, m)], 1, 1)
        dk0 = dot(q, top, 1, 1)
        dk1 = dot(q[:, m:], low, 1, 1)
        dq0 = dot(k[:, :m], top[:, :m])
        dq1 = dot(k, jnp.concatenate([top[:, m:], low], axis=0))
        for kind, grad in (
            (1, jnp.concatenate([dv0, dv1], axis=1)),
            (2, jnp.concatenate([dq0, dq1], axis=1) * (scale * 0.5)),
            (3, jnp.concatenate([dk0, dk1], axis=1)),
        ):
            to = pl.ds(kind * features + h * size, size)
            dp_ref[to, :] = (grad * slope_ref[to, :]).astype(BF16)

    d_normed = (dot(w_ref[...], dp_ref[...]) * 0.5).astype(BF16).astype(F32)
    normed, inv = norm_parts(x_ref[...].astype(F32))
    back = norm_back(d_normed, normed, inv).astype(BF16).astype(F32)
    dx_ref[...] = (back + g_ref[...].astype(F32)).astype(BF16)

    place = place_ref[...]
    y_ref[...] = dot(y_ref[...], place).astype(BF16)
    dx_ref[...] = dot(dx_ref[...], place).astype(BF16)
    for t in range(tables):
        at = pl.ds(t * c, c)
        out_ref[pl.ds(t * m, m), :] = to_blocks(y_ref[at, :], dx_ref[at, :])


def vmem(n):
    return [pl.BlockSpec(memory_space=pltpu.VMEM)] * n


def inverse(plan):
    n = plan.shape[-1]
    index = jnp.arange(n, dtype=jnp.int32)
    hit = plan[..., :, None] == index
    return jnp.sum(jnp.where(hit, index[:, None], 0), axis=-2)


def layer(blocks, pick, place, far, slopes, uvqk_weight, out_weight):
    features = uvqk_weight.shape[0]
    heads = slopes.shape[0]
    rows = pick.shape[0]
    wide = pltpu.VMEM((features, rows), F32)
    thin = pltpu.VMEM((features, rows), BF16)
    return pl.pallas_call(
        layer_kernel,
        out_shape=jax.ShapeDtypeStruct(blocks.shape, BF16),
        in_specs=[pl.BlockSpec(memory_space=pltpu.SMEM)] + vmem(8),
        out_specs=pl.BlockSpec(memory_space=pltpu.VMEM),
        scratch_shapes=[
            thin, thin, pltpu.VMEM((4 * features, rows), F32), wide, thin, thin, thin,
            pltpu.VMEM((heads, rows, rows), BF16), pltpu.VMEM((heads, rows, rows), F32),
            wide, pltpu.VMEM((4 * features, rows), BF16), thin, thin,
        ],
        name="layer",
    )(
        slopes, blocks, pick, place, far,
        (uvqk_weight * jnp.asarray(0.5, BF16)).T, uvqk_weight, out_weight.T, out_weight,
    )


def tables_of(own_work, lengths, rows):
    peers = rows // TILE
    m = peers * HALF
    lane = jnp.arange(rows, dtype=jnp.int32)
    inner = lane % TILE
    spot = jnp.repeat(own_work, TILE) * HALF + inner % HALF + (inner // HALF) * m
    pick = (lane[:, None] == spot[None, :]).astype(BF16)
    place = (spot[:, None] == lane[None, :]).astype(BF16)
    bound = jnp.cumsum(lengths)
    segment = jnp.sum(((lane // TILE)[None, :] >= bound[:, None]).astype(jnp.int32), axis=0)
    seen = (segment[:, None] == segment[None, :]) & (lane[:, None] <= lane[None, :])
    return pick, place, jnp.where(seen, 0.0, FAR).astype(F32)


def shards(
    embeds, cotangent, send_plan, work_plan, sequence_tiles, slopes, uvqk_weight, out_weight
):
    tables = lax.axis_size("table")
    peers = lax.axis_size("replica")
    columns = embeds.shape[1]
    rows = embeds.shape[0] // tables
    plan = send_plan[0]
    sent = jax.ShapeDtypeStruct((tables * peers * HALF, 4 * columns), BF16)
    axes = ("table", "replica")
    blocks = pl.pallas_call(
        send_kernel, out_shape=sent, in_specs=vmem(3),
        out_specs=pl.BlockSpec(memory_space=pltpu.VMEM), name="send",
    )(plan, embeds.T, cotangent.T)

    def exchange(a):
        a = a.reshape(tables * peers, HALF, 4 * columns)
        a = lax.all_to_all(a, axes, split_axis=0, concat_axis=0, tiled=True)
        return a.reshape(sent.shape)

    pick, place, far = tables_of(work_plan[0, 0], sequence_tiles[0, 0], rows)
    done = layer(exchange(blocks), pick, place, far, slopes, uvqk_weight, out_weight)
    home = jax.ShapeDtypeStruct((columns, tables * rows), BF16)
    y, d = pl.pallas_call(
        home_kernel, out_shape=(home, home), in_specs=vmem(2),
        out_specs=(pl.BlockSpec(memory_space=pltpu.VMEM),) * 2, name="home",
    )(inverse(plan), exchange(done))
    return y.T, d.T


def solution(mesh):
    in_specs = (
        P("replica", "table"),
        P("replica", "table"),
        P("replica", None, None),
        P("replica", "table", None),
        P("replica", "table", None),
        P(),
        P(),
        P(),
    )
    out_specs = (P("replica", "table"), P("replica", "table"))
    return jax.shard_map(shards, mesh=mesh, in_specs=in_specs, out_specs=out_specs, check_vma=False)
```

time: 190 us -> 123 us (0.65)
  local copies, waits for them, and re-layouts: 29.8 us -> 5.27 us
  matrix products: 22.9 us -> 0 us
  starting transfers between devices: 52.9 us -> 32.8 us
  Pallas kernels: 0 us -> 16.3 us
  waiting for transfers between devices: 76.9 us -> 61.7 us
    dot_general x52 -> x0, matrix products: 22.9 us -> none  [the longest x24 10.5 us: hstu_layer(): jnp.dot(query_part[:, lower:upper], key_part[:, lower:upper].T, preferred...]
    all_to_all x8 -> x2, starting transfers between devices: 52.9 us -> 32.8 us  [exchange(): a = lax.all_to_all(a, axes, split_axis=0, concat_axis=0, tiled=True)]
    pallas_call x0 -> x3, Pallas kernels: none -> 16.3 us  [the longest x1 10.8 us: layer(): pl.pallas_call(layer_kernel, out_shape=jax.ShapeDtypeStruct(blocks.shape,...]
    all_to_all x8 -> x2, waiting for transfers between devices: 76.9 us -> 61.7 us  [exchange(): a = lax.all_to_all(a, axes, split_axis=0, concat_axis=0, tiled=True)]
    all_to_all x10 -> x0, local copies, waits for them, and re-layouts: 13 us -> none  [the longest x3 3.8 us: shards(): lax.all_to_all(to_home(back_grads), 'table', split_axis=1, concat_axis=0,...]
    gather x8 -> x0, local copies, waits for them, and re-layouts: 10.5 us -> none  [the longest x2 3.04 us: to_home(): return result[undo_send].reshape(row_count, feature_count)]
    transpose x0 -> x1, other arithmetic: none -> 3.1 us  [layer(): return pl.pallas_call(layer_kernel, out_shape=jax.ShapeDtypeStruct(blocks...]
    unnamed x84 -> x16, local copies, waits for them, and re-layouts: 2.06 us -> 5.12 us
  transfers between devices with their start and end apart: 8 -> 2, of which waited for: 8 -> 2; matrix products, arithmetic and copies ran while one was open for 20% -> 8% of each run, Pallas kernels for 0% -> 0%
where the time goes in v1:
time: 123 us
  waiting for transfers between devices  61.7 us (50%)
  starting transfers between devices  32.8 us (27%)
  Pallas kernels  16.3 us (13%)
  other arithmetic  5.69 us (5%)
  local copies, waits for them, and re-layouts  5.27 us (4%)
    all_to_all x2, waiting for transfers between devices, exchange(): a = lax.all_to_all(a, axes, split_axis=0, concat_axis=0, tiled=True)  61.7 us
    all_to_all x2, starting transfers between devices, exchange(): a = lax.all_to_all(a, axes, split_axis=0, concat_axis=0, tiled=True)  32.8 us
    pallas_call x1, Pallas kernels, layer(): pl.pallas_call(layer_kernel, out_shape=jax.ShapeDtypeStruct(blocks.shape,...  10.8 us
    unnamed x16, local copies, waits for them, and re-layouts  5.12 us
    transpose x1, other arithmetic, layer(): return pl.pallas_call(layer_kernel, out_shape=jax.ShapeDtypeStruct(blocks...  3.1 us
    pallas_call x1, Pallas kernels, shards(): pl.pallas_call(send_kernel, out_shape=sent, in_specs=vmem(3), out_specs=p...  3.04 us
  transfers between devices with their start and end apart: 2, of which 2 were waited for; matrix products, arithmetic and copies ran while one was open for 8% of the time, Pallas kernels for 0%

profile of v1, /device:TPU:1, one launch (start us, length us, event | category | flops | bytes accessed | tf_op | source)
XLA Modules:
  0.0 122.6 jit_solution(10477807376593392796)
XLA Ops:
  0.6 0.0 copy-start.5
  0.6 0.0 copy-start
  0.7 3.0 %send.1 = bf16[2048,128]{1,0:T(8,128)(2,1)} custom-call(s32[16,32]{1,0:T(8,128)} %bitcast.23, bf16[32,4096]{1,0:T(8,128)(2,1)} %bitcast.21, bf16[32,4096]{1,0:T(8,128)(2,1)} %bitcast.22), custom_call_target="tpu_custom_call" | custom-call | tf_op jit(solution)/shard_map/send/pallas_call | solution.py:258
  3.7 24.3 %all-to-all-start = ((bf16[512,4,128]{2,1,0:T(4,128)(2,1)}), bf16[512,4,128]{2,1,0:T(4,128)(2,1)S(1)}, u32[]{:S(2)}, u32[]{:S(2)}) async-start(bf16[512,4,128]{2,1,0:T(4,128)(2,1)} %bitcast.16), calls=%async_computation | async-start | bytes 1048576 | tf_op jit(solution)/shard_map/all_to_all | solution.py:265
  28.0 0.0 copy-done.5
  28.0 0.1 broadcast_in_dim.20
  28.1 0.1 mul.46
  28.2 0.0 copy-done
  28.2 0.0 copy-start.2
  28.2 0.0 copy-start.6
  28.2 2.5 %copy.14 = bf16[512,2048]{0,1:T(8,128)(2,1)} copy(bf16[512,2048]{1,0:T(8,128)(2,1)S(1)} %copy-done) | data formatting | bytes 4194304 | tf_op args[6]
  30.7 0.0 copy-done.2
  30.7 1.0 copy.15
  31.7 0.0 copy-done.6
  31.7 0.2 reduce-window.8
  31.9 0.1 convert_reduce_fusion
  32.0 0.8 fusion.1
  32.8 0.8 fusion.3.far_ref
  33.6 3.1 %multiply_bitcast_fusion.wt_ref = bf16[2048,512]{1,0:T(8,128)(2,1)} fusion(bf16[512,2048]{0,1:T(8,128)(2,1)} %copy.14), kind=kLoop, calls=%fused_computation | loop fusion | flops 1048576 | bytes 4194304 | tf_op jit(solution)/shard_map/transpose | solution.py:230
  36.7 27.0 %all-to-all-done = bf16[512,4,128]{2,1,0:T(4,128)(2,1)S(1)} async-done(((bf16[512,4,128]{2,1,0:T(4,128)(2,1)}), bf16[512,4,128]{2,1,0:T(4,128)(2,1)S(1)}, u32[]{:S(2)}, u32[]{:S(2)}) %all-to-all-start) | async-done | bytes 524320 | tf_op jit(solution)/shard_map/all_to_all | solution.py:265
  63.6 0.0 copy-start.3
  63.6 0.8 copy-done.3
  64.4 0.0 copy-start.4
  64.4 10.8 %layer.1 = bf16[2048,128]{1,0:T(8,128)(2,1)} custom-call(f32[8]{0:T(128)} %slopes_ref.1, bf16[2048,128]{1,0:T(8,128)(2,1)} %bitcast.18, bf16[256,256]{1,0:T(8,128)(2,1)} %get-tuple-element.7.pick_ref, bf16[256,256]{1,0:T(8,128)(2,1)} %get-tuple-element.6.place_ref, f32[256,256]{1,0:T(8,128)} %fusion.3.far_ref, ...), custom_call_target="tpu_custom_call" | custom-call | tf_op jit(solution)/shard_map/layer/pallas_call | solution.py:217
  75.2 8.6 %all-to-all-start.1 = ((bf16[512,4,128]{2,1,0:T(4,128)(2,1)}), bf16[512,4,128]{2,1,0:T(4,128)(2,1)S(1)}, u32[]{:S(2)}, u32[]{:S(2)}) async-start(bf16[512,4,128]{2,1,0:T(4,128)(2,1)} %bitcast.20), calls=%async_computation.1 | async-start | bytes 1048576 | tf_op jit(solution)/shard_map/all_to_all | solution.py:265
  83.8 0.0 copy-done.4
  83.8 0.7 select_reduce_fusion.back_ref
  84.6 34.8 %all-to-all-done.1 = bf16[512,4,128]{2,1,0:T(4,128)(2,1)S(1)} async-done(((bf16[512,4,128]{2,1,0:T(4,128)(2,1)}), bf16[512,4,128]{2,1,0:T(4,128)(2,1)S(1)}, u32[]{:S(2)}, u32[]{:S(2)}) %all-to-all-start.1) | async-done | bytes 524320 | tf_op jit(solution)/shard_map/all_to_all | solution.py:265
  119.4 0.0 copy-start.1
  119.4 0.8 copy-done.1
  120.2 2.5 %home.1 = (bf16[32,4096]{1,0:T(8,128)(2,1)}, bf16[32,4096]{1,0:T(8,128)(2,1)}) custom-call(s32[16,32]{1,0:T(8,128)} %select_reduce_fusion.back_ref, bf16[2048,128]{1,0:T(8,128)(2,1)} %bitcast.17), custom_call_target="tpu_custom_call" | custom-call | tf_op jit(solution)/shard_map/home/pallas_call | solution.py:271
  (3 shorter events, 0.0 us)
Async XLA Ops:
  0.6 27.4 %copy-start.5 = (s32[1,1,32]{2,1,0:T(1,128)S(1)}, s32[1,1,32]{2,1,0:T(1,128)}, u32[]{:S(2)}) copy-start(s32[1,1,32]{2,1,0:T(1,128)} %param.11) | copy-start | bytes 388
  0.6 27.5 %copy-start = (bf16[512,2048]{1,0:T(8,128)(2,1)S(1)}, bf16[512,2048]{1,0:T(8,128)(2,1)}, u32[]{:S(2)}) copy-start(bf16[512,2048]{1,0:T(8,128)(2,1)} %w_ref.1) | copy-start | bytes 6291460
  3.7 59.9 %all-to-all-start = ((bf16[512,4,128]{2,1,0:T(4,128)(2,1)}), bf16[512,4,128]{2,1,0:T(4,128)(2,1)S(1)}, u32[]{:S(2)}, u32[]{:S(2)}) async-start(bf16[512,4,128]{2,1,0:T(4,128)(2,1)} %bitcast.16), calls=%async_computation | async-start | bytes 1048576 | tf_op jit(solution)/shard_map/all_to_all | solution.py:265
  28.2 2.5 %copy-start.2 = (bf16[512,512]{1,0:T(8,128)(2,1)S(1)}, bf16[512,512]{1,0:T(8,128)(2,1)}, u32[]{:S(2)}) copy-start(bf16[512,512]{1,0:T(8,128)(2,1)} %o_ref.1) | copy-start | bytes 1572868
  28.2 3.5 %copy-start.6 = (s32[1,1,4]{2,1,0:T(1,128)S(1)}, s32[1,1,4]{2,1,0:T(1,128)}, u32[]{:S(2)}) copy-start(s32[1,1,4]{2,1,0:T(1,128)} %param.12) | copy-start | bytes 52
  63.6 0.8 copy-start.3
  64.4 19.4 %copy-start.4 = (s32[1,16,32]{2,1,0:T(8,128)S(1)}, s32[1,16,32]{2,1,0:T(8,128)}, u32[]{:S(2)}) copy-start(s32[1,16,32]{2,1,0:T(8,128)} %param.10) | copy-start | bytes 6148
  75.2 44.1 %all-to-all-start.1 = ((bf16[512,4,128]{2,1,0:T(4,128)(2,1)}), bf16[512,4,128]{2,1,0:T(4,128)(2,1)S(1)}, u32[]{:S(2)}, u32[]{:S(2)}) async-start(bf16[512,4,128]{2,1,0:T(4,128)(2,1)} %bitcast.20), calls=%async_computation.1 | async-start | bytes 1048576 | tf_op jit(solution)/shard_map/all_to_all | solution.py:265
  119.4 0.8 copy-start.1
